TPU v7x, 32 devices: a whole 2x2x4 slice. The times are simulated.
32 devices in a mesh: spatial: 8 (over z, x), filter: 4 (over y, core).
Axes of the slice: x: 2, y: 2, z: 4, core: 2. Of those that a mesh axis runs over, the one named last changes fastest.
Arguments:
- volume_in: bfloat16 [128, 32, 8192], P('filter', 'spatial'), may hold values from -6 to 6
- filters_a: bfloat16 [27, 256, 128], P(None, 'filter'), may hold values from -0.109375 to 0.109375
- bias_a: bfloat16 [256], P('filter'), may hold values from -0.5 to 0.5
- filters_b: bfloat16 [27, 256, 256], P(None, 'filter'), may hold values from -0.078125 to 0.078125
- bias_b: bfloat16 [256], P('filter'), may hold values from -0.5 to 0.5
Outputs:
- volume_out: bfloat16 [256, 8, 512], P('filter', 'spatial')
All inputs are finite; a program needn't handle non-finite values.
Results may differ from a plain program's by a relative error of at most 0.0048.
Values may be sent and summed in bfloat16 or wider, within the bound.
A program may use at most 128 MiB of HBM per device.

v0:
```python
import jax
import jax.numpy as jnp
from jax import lax
from jax.sharding import PartitionSpec as P

ROWS = 64
COLS = 128


def shifted(block, axis, distance):
    devices = range(lax.axis_size(axis))
    route = [(i - distance, i) for i in devices if i - distance in devices]
    return lax.ppermute(block, axis, route)


def local_conv(block, weight, pad_rows, row_count, col_count):
    channels = block.shape[0]
    slices = block.shape[1]
    volume = block.reshape(1, channels, slices, row_count, col_count)
    kernel = weight.reshape(3, 3, 3, weight.shape[1], weight.shape[2])
    return lax.conv_general_dilated(
        volume,
        kernel,
        (2, 2, 2),
        ((0, 0), (pad_rows, pad_rows), (1, 1)),
        dimension_numbers=("NCDHW", "DHWOI", "NCDHW"),
        preferred_element_type=jnp.float32,
    )[0]


def activate(summed, bias_vec):
    summed = summed + bias_vec.astype(jnp.float32)[:, None, None, None]
    return jnp.where(summed > 0, summed, 0.2 * summed).astype(jnp.bfloat16)


def per_device(volume_in, filters_a, bias_a, filters_b, bias_b):
    slices = volume_in.shape[1]
    outputs = filters_a.shape[1]
    beneath = shifted(volume_in[:, -1:], "spatial", 1)
    extended = jnp.concatenate([beneath, volume_in], 1)
    zeros_first = jnp.zeros((outputs, slices // 2, ROWS // 2, COLS // 2), jnp.float32)
    weight_part = filters_a
    summed = zeros_first + local_conv(
        lax.all_gather(extended, "filter", axis=0, tiled=True), weight_part, 1, ROWS, COLS
    )
    hidden = activate(summed, bias_a).reshape(outputs, slices // 2, ROWS // 2 * (COLS // 2))
    beneath_two = shifted(hidden[:, -1:], "spatial", 1)
    extended_two = jnp.concatenate([beneath_two, hidden], 1)
    zeros_second = jnp.zeros((filters_b.shape[1], slices // 4, ROWS // 4, COLS // 4), jnp.float32)
    weight_part = filters_b
    summed_two = zeros_second + local_conv(
        lax.all_gather(extended_two, "filter", axis=0, tiled=True),
        weight_part,
        1,
        ROWS // 2,
        COLS // 2,
    )
    return activate(summed_two, bias_b).reshape(
        filters_b.shape[1], slices // 4, ROWS // 4 * (COLS // 4)
    )


def solution(mesh):
    in_specs = (
        P("filter", "spatial", None),
        P(None, "filter", None),
        P("filter"),
        P(None, "filter", None),
        P("filter"),
    )
    out_specs = P("filter", "spatial", None)
    return jax.shard_map(
        per_device, mesh=mesh, in_specs=in_specs, out_specs=out_specs, check_vma=False
    )
```

profile of v0, /device:TPU:0, one launch (start us, length us, event | category | flops | bytes accessed | tf_op | source)
XLA Modules:
  0.0 223.8 jit_solution(5031182525449573084)
XLA Ops:
  6.5 0.0 copy-start
  6.5 0.0 all-gather.3.cloned.1.call-start
  6.5 2.8 %copy.46 = bf16[32,4,8192]{2,0,1:T(8,128)(2,1)S(1)} copy(bf16[32,4,8192]{2,1,0:T(4,128)(2,1)} %param.5) | data formatting | bytes 4194304 | tf_op args[0]
  9.4 0.0 copy-start.2
  9.4 4.9 %collective-permute-start = (bf16[32,1,8192]{2,0,1:T(8,128)(2,1)S(1)}, bf16[32,1,8192]{2,0,1:T(8,128)(2,1)S(1)}, u32[]{:S(2)}, u32[]{:S(2)}) collective-permute-start(bf16[32,1,8192]{2,0,1:T(8,128)(2,1)S(1)} %slice.12), channel_id=1, source_target_pairs={{0,4},{4,8},{8,12},{12,16},{16,20},{20,24},{24,28},{1,5},{5,9},{9,... | collective-permute-start | bytes 1572872 | tf_op jit(solution)/shard_map/ppermute | solution.py:13
  14.3 11.1 %collective-permute-done = bf16[32,1,8192]{2,0,1:T(8,128)(2,1)S(1)} collective-permute-done((bf16[32,1,8192]{2,0,1:T(8,128)(2,1)S(1)}, bf16[32,1,8192]{2,0,1:T(8,128)(2,1)S(1)}, u32[]{:S(2)}, u32[]{:S(2)}) %collective-permute-start) | collective-permute-done | bytes 524320 | tf_op jit(solution)/shard_map/ppermute | solution.py:13
  25.4 1.8 pad_maximum_fusion
  27.2 0.0 all-gather.3.cloned.1.call-update
  27.2 0.0 all-gather.5.cloned.1.call-start
  27.3 0.0 copy-done.2
  27.3 72.5 %all-gather.3.cloned.1.call-done = bf16[128,5,8192]{2,0,1:T(8,128)(2,1)} async-done(((bf16[32,5,8192]{2,0,1:T(8,128)(2,1)}), bf16[128,5,8192]{2,0,1:T(8,128)(2,1)}) %all-gather.3.cloned.1.call-update) | async-done | bytes 10485776 | tf_op jit(solution)/shard_map/all_gather | solution.py:44
  99.8 14.2 %copy.48 = bf16[128,5,8192]{0,2,1:T(8,128)(2,1)} copy(bf16[128,5,8192]{2,0,1:T(8,128)(2,1)} %all-gather.3.cloned.1.call-done) | data formatting | bytes 20971520 | tf_op jit(solution)/shard_map/all_gather | solution.py:44
  114.0 14.7 %copy.61 = bf16[128,5,64,1,128]{0,2,4,1,3:T(8,128)(2,1)} copy(bf16[128,5,64,1,128]{0,4,2,1,3:T(8,128)(2,1)} %bitcast.31) | data formatting | bytes 20971520
  128.8 6.4 %pad.clone = bf16[128,5,64,1,144]{0,2,4,1,3:T(8,128)(2,1)S(1)} pad(bf16[128,5,64,1,128]{0,2,4,1,3:T(8,128)(2,1)} %copy.61, bf16[]{:T(256)} %constant.1), padding=0_0x0_0x0_0x0_0x1_15 | pad | bytes 22282242 | tf_op jit(solution)/shard_map/reshape | solution.py:19
  135.2 0.0 copy-start.1
  135.2 0.0 copy-start.4
  135.2 8.6 %copy.51 = bf16[128,5,64,1,8,18]{0,4,5,2,1,3:T(8,128)(2,1)S(1)} copy(bf16[128,5,64,1,8,18]{0,2,5,4,1,3:T(8,128)(2,1)S(1)} %bitcast.30) | data formatting | bytes 23592960 | tf_op jit(solution)/shard_map/conv_general_dilated | solution.py:21
  143.9 0.3 slice.13
  144.2 0.0 copy-done.1
  144.2 0.0 copy-done.4
  144.2 10.2 %fusion.12 = f32[2,32,8,9,64]{4,2,3,1,0:T(8,128)} fusion(bf16[3,3,3,64,128]{4,3,2,1,0:T(8,128)(2,1)S(1)} %bitcast.37, bf16[128,5,64,1,7,2]{0,4,5,2,1,3:T(8,128)(2,1)S(1)} %slice.13, bf16[128,5,64,1,8,18]{0,4,5,2,1,3:T(8,128)(2,1)S(1)} %copy.51, pred[8,9]{0,1:T(8,128)(4,1)S(1)} %copy-done.4), kind=kOutput, calls=%fused_computation.15 | convolution fusion | flops 2056814592 | bytes 14565448 | tf_op jit(solution)/shard_map/conv_general_dilated | solution.py:21
  154.5 2.1 copy.52
  156.6 0.2 slice_bitcast_fusion
  156.8 3.1 %copy.53 = f32[1,64,2,32,64]{4,3,1,2,0:T(8,128)} copy(f32[1,64,2,32,64]{1,3,4,2,0:T(8,128)S(1)} %slice_bitcast_fusion) | data formatting | bytes 2097152 | tf_op jit(solution)/shard_map/conv_general_dilated | solution.py:21
  159.8 0.0 copy-start.3
  159.8 2.1 squeeze.6
  161.9 0.2 fusion.18
  162.2 3.4 %collective-permute-start.1 = (bf16[64,1,2048]{2,0,1:T(8,128)(2,1)S(1)}, bf16[64,1,2048]{2,0,1:T(8,128)(2,1)S(1)}, u32[]{:S(2)}, u32[]{:S(2)}) collective-permute-start(bf16[64,1,2048]{2,0,1:T(8,128)(2,1)S(1)} %slice.15), channel_id=1, source_target_pairs={{0,4},{4,8},{8,12},{12,16},{16,20},{20,24},{24,28},{1,5},{5,9},{9,... | collective-permute-start | bytes 786440 | tf_op jit(solution)/shard_map/ppermute | solution.py:13
  165.6 6.0 %collective-permute-done.1 = bf16[64,1,2048]{2,0,1:T(8,128)(2,1)S(1)} collective-permute-done((bf16[64,1,2048]{2,0,1:T(8,128)(2,1)S(1)}, bf16[64,1,2048]{2,0,1:T(8,128)(2,1)S(1)}, u32[]{:S(2)}, u32[]{:S(2)}) %collective-permute-start.1) | collective-permute-done | bytes 262176 | tf_op jit(solution)/shard_map/ppermute | solution.py:13
  171.5 1.0 pad_maximum_fusion.1
  172.5 0.0 all-gather.5.cloned.1.call-update
  172.5 0.0 copy-done.3
  172.6 29.7 %all-gather.5.cloned.1.call-done = bf16[256,3,2048]{2,0,1:T(8,128)(2,1)} async-done(((bf16[64,3,2048]{2,0,1:T(8,128)(2,1)}), bf16[256,3,2048]{2,0,1:T(8,128)(2,1)}) %all-gather.5.cloned.1.call-update) | async-done | bytes 3145744 | tf_op jit(solution)/shard_map/all_gather | solution.py:52
  202.2 4.6 %copy.54 = bf16[256,3,2048]{0,2,1:T(8,128)(2,1)} copy(bf16[256,3,2048]{2,0,1:T(8,128)(2,1)} %all-gather.5.cloned.1.call-done) | data formatting | bytes 6291456 | tf_op jit(solution)/shard_map/all_gather | solution.py:52
  206.9 3.7 %copy.62 = bf16[256,3,32,1,64]{0,2,4,1,3:T(8,128)(2,1)S(1)} copy(bf16[256,3,32,1,64]{0,4,2,1,3:T(8,128)(2,1)} %bitcast.33) | data formatting | bytes 6291456
  210.6 0.4 pad.2.clone
  211.0 0.0 copy-start.5
  211.0 2.3 %copy.57 = bf16[256,3,32,1,8,10]{0,4,5,2,1,3:T(8,128)(2,1)S(1)} copy(bf16[256,3,32,1,8,10]{0,2,5,4,1,3:T(8,128)(2,1)S(1)} %bitcast.32) | data formatting | bytes 7864320 | tf_op jit(solution)/shard_map/conv_general_dilated | solution.py:21
  213.3 0.2 slice.16
  213.5 0.0 copy-done
  213.5 0.0 copy-done.5
  213.5 2.5 %fusion.15 = f32[1,16,8,5,64]{4,2,3,1,0:T(8,128)S(1)} fusion(bf16[3,3,3,64,256]{4,3,2,1,0:T(8,128)(2,1)S(1)} %bitcast.29, bf16[256,3,32,1,7,2]{0,4,5,2,1,3:T(8,128)(2,1)S(1)} %slice.16, bf16[256,3,32,1,8,10]{0,4,5,2,1,3:T(8,128)(2,1)S(1)} %copy.57, pred[8,5]{0,1:T(8,128)(4,1)S(1)} %copy-done.5), kind=kOutput, calls=%fused_computation.16 | convolution fusion | flops 568631296 | bytes 5668904 | tf_op jit(solution)/shard_map/conv_general_dilated | solution.py:21
  216.0 0.1 copy.58
  216.1 0.1 copy.59
  216.1 0.1 copy.60
  216.3 0.7 fusion.19
  (5 shorter events, 0.1 us)
Async XLA Ops:
  6.5 206.9 %copy-start = (bf16[27,64,256]{2,1,0:T(8,128)(2,1)S(1)}, bf16[27,64,256]{2,1,0:T(8,128)(2,1)}, u32[]{:S(2)}) copy-start(bf16[27,64,256]{2,1,0:T(8,128)(2,1)} %param.8) | copy-start | bytes 2654212
  6.5 93.3 %all-gather.3.cloned.1.call-start = ((), (), s32[]{:S(2)}) async-start(), calls=%async_computation | async-start | bytes 13107200 | tf_op jit(solution)/shard_map/all_gather | solution.py:44
  9.4 17.9 %copy-start.2 = (bf16[64]{0:T(256)(128)(2,1)S(1)}, bf16[64]{0:T(256)(128)(2,1)}, u32[]{:S(2)}) copy-start(bf16[64]{0:T(256)(128)(2,1)} %param.7) | copy-start | bytes 388
  9.4 16.0 %collective-permute-start = (bf16[32,1,8192]{2,0,1:T(8,128)(2,1)S(1)}, bf16[32,1,8192]{2,0,1:T(8,128)(2,1)S(1)}, u32[]{:S(2)}, u32[]{:S(2)}) collective-permute-start(bf16[32,1,8192]{2,0,1:T(8,128)(2,1)S(1)} %slice.12), channel_id=1, source_target_pairs={{0,4},{4,8},{8,12},{12,16},{16,20},{20,24},{24,28},{1,5},{5,9},{9,... | collective-permute-start | bytes 1572872 | tf_op jit(solution)/shard_map/ppermute | solution.py:13
  27.2 175.0 %all-gather.5.cloned.1.call-start = ((), (), s32[]{:S(2)}) async-start(), calls=%async_computation.1 | async-start | bytes 3932160 | tf_op jit(solution)/shard_map/all_gather | solution.py:52
  135.2 9.0 %copy-start.1 = (bf16[27,64,128]{2,1,0:T(8,128)(2,1)S(1)}, bf16[27,64,128]{2,1,0:T(8,128)(2,1)}, u32[]{:S(2)}) copy-start(bf16[27,64,128]{2,1,0:T(8,128)(2,1)} %param.6) | copy-start | bytes 1327108
  135.2 9.0 %copy-start.4 = (pred[8,9]{0,1:T(8,128)(4,1)S(1)}, pred[8,9]{0,1:T(8,128)(4,1)}, u32[]{:S(2)}) copy-start(pred[8,9]{0,1:T(8,128)(4,1)} %constant.16) | copy-start | bytes 220
  159.8 12.7 %copy-start.3 = (bf16[64]{0:T(256)(128)(2,1)S(1)}, bf16[64]{0:T(256)(128)(2,1)}, u32[]{:S(2)}) copy-start(bf16[64]{0:T(256)(128)(2,1)} %param.9) | copy-start | bytes 388
  162.2 9.4 %collective-permute-start.1 = (bf16[64,1,2048]{2,0,1:T(8,128)(2,1)S(1)}, bf16[64,1,2048]{2,0,1:T(8,128)(2,1)S(1)}, u32[]{:S(2)}, u32[]{:S(2)}) collective-permute-start(bf16[64,1,2048]{2,0,1:T(8,128)(2,1)S(1)} %slice.15), channel_id=1, source_target_pairs={{0,4},{4,8},{8,12},{12,16},{16,20},{20,24},{24,28},{1,5},{5,9},{9,... | collective-permute-start | bytes 786440 | tf_op jit(solution)/shard_map/ppermute | solution.py:13
  211.0 2.5 %copy-start.5 = (pred[8,5]{0,1:T(8,128)(4,1)S(1)}, pred[8,5]{0,1:T(8,128)(4,1)}, u32[]{:S(2)}) copy-start(pred[8,5]{0,1:T(8,128)(4,1)} %constant.15) | copy-start | bytes 124
Sparse Core Ops, SparseCore 0:
  27.4 72.4 all-gather.2
  172.7 29.5 all-gather.4
where the time goes:
time: 225 us; the launch traced here: 224 us
  waiting for transfers between devices  119 us (53%)
  local copies, waits for them, and re-layouts  66.2 us (29%)
  between operations  13.6 us (6%)
  matrix products  12.7 us (6%)
  starting transfers between devices  8.31 us (4%)
  other arithmetic  3.7 us (2%)
    all_gather x1, waiting for transfers between devices, per_device(): lax.all_gather(extended, 'filter', axis=0, tiled=True)  72.5 us
    all_gather x1, waiting for transfers between devices, per_device(): lax.all_gather(extended_two, 'filter', axis=0, tiled=True)  29.7 us
    unnamed x15, local copies, waits for them, and re-layouts  21.3 us
    ppermute x2, waiting for transfers between devices, shifted(): return lax.ppermute(block, axis, route)  17.1 us
    conv_general_dilated x10, local copies, waits for them, and re-layouts, local_conv(): lax.conv_general_dilated(volume, kernel, (2, 2, 2), ((0, 0), (pad_rows, p...  17 us
    all_gather x1, local copies, waits for them, and re-layouts, per_device(): lax.all_gather(extended, 'filter', axis=0, tiled=True)  14.2 us
    conv_general_dilated x2, matrix products, local_conv(): lax.conv_general_dilated(volume, kernel, (2, 2, 2), ((0, 0), (pad_rows, p...  12.7 us
    ppermute x2, starting transfers between devices, shifted(): return lax.ppermute(block, axis, route)  8.26 us
  transfers between devices with their start and end apart: 4, of which 4 were waited for; matrix products, arithmetic and copies ran while one was open for 0% of the time, Pallas kernels for 0%

commit v1 on v0

--- a/solution.py
+++ b/solution.py
@@ -40,8 +40,25 @@
     extended = jnp.concatenate([beneath, volume_in], 1)
     zeros_first = jnp.zeros((outputs, slices // 2, ROWS // 2, COLS // 2), jnp.float32)
     weight_part = filters_a
+
+    def turn_the_things(vec, axis_id):
+        parts_out, far_arr = (lax.axis_size(axis_id), lax.axis_index(axis_id))
+        g_now, local_next = (vec, 1)
+        while local_next < parts_out:
+            ledger = []
+            d = 0
+            while d < parts_out:
+                ledger.append((d, d ^ local_next))
+                d += 1
+            val = lax.ppermute(g_now, axis_name=axis_id, perm=ledger)
+            last = jnp.concatenate([g_now, val], axis=0)
+            high = jnp.concatenate([val, g_now], axis=0)
+            g_now = jnp.where(far_arr & local_next == 0, last, high)
+            local_next = 2 * local_next
+        return g_now
+
     summed = zeros_first + local_conv(
-        lax.all_gather(extended, "filter", axis=0, tiled=True), weight_part, 1, ROWS, COLS
+        turn_the_things(extended, "filter"), weight_part, 1, ROWS, COLS
     )
     hidden = activate(summed, bias_a).reshape(outputs, slices // 2, ROWS // 2 * (COLS // 2))
     beneath_two = shifted(hidden[:, -1:], "spatial", 1)

time: 225 us -> 278 us (1.24)
  waiting for transfers between devices: 119 us -> 159 us
  other arithmetic: 3.7 us -> 18.3 us
  local copies, waits for them, and re-layouts: 66.2 us -> 63.1 us
    ppermute x0 -> x2, waiting for transfers between devices: none -> 111 us  [turn_the_things(): val = lax.ppermute(g_now, axis_name=axis_id, perm=ledger)]
    all_gather x1 -> x0, waiting for transfers between devices: 72.5 us -> none  [per_device(): lax.all_gather(extended, 'filter', axis=0, tiled=True)]
    all_gather x1 -> x0, local copies, waits for them, and re-layouts: 14.2 us -> none  [per_device(): lax.all_gather(extended, 'filter', axis=0, tiled=True)]
    select_n x0 -> x2, other arithmetic: none -> 11.4 us  [turn_the_things(): g_now = jnp.where(far_arr & local_next == 0, last, high)]
    unnamed x15 -> x21, local copies, waits for them, and re-layouts: 21.3 us -> 28.2 us
    reshape x2 -> x1, local copies, waits for them, and re-layouts: 6.84 us -> 0.42 us  [local_conv(): volume = block.reshape(1, channels, slices, row_count, col_count)]
    select_n x0 -> x1, local copies, waits for them, and re-layouts: none -> 6.43 us  [turn_the_things(): g_now = jnp.where(far_arr & local_next == 0, last, high)]
    concatenate x1, other arithmetic: 1.78 us -> 4.89 us  [turn_the_things(): last = jnp.concatenate([g_now, val], axis=0)]
  transfers between devices with their start and end apart: 4 -> 5, of which waited for: 4 -> 5; matrix products, arithmetic and copies ran while one was open for 0% -> 3% of each run, Pallas kernels for 0% -> 0%
where the time goes in v1:
time: 278 us; the launch traced here: 277 us
  waiting for transfers between devices  159 us (57%)
  local copies, waits for them, and re-layouts  63.1 us (23%)
  other arithmetic  18.3 us (7%)
  between operations  13.7 us (5%)
  matrix products  12.7 us (5%)
  starting transfers between devices  10.9 us (4%)
    ppermute x2, waiting for transfers between devices, turn_the_things(): val = lax.ppermute(g_now, axis_name=axis_id, perm=ledger)  111 us
    all_gather x1, waiting for transfers between devices, per_device(): lax.all_gather(extended_two, 'filter', axis=0, tiled=True)  31.8 us
    unnamed x21, local copies, waits for them, and re-layouts  28.2 us
    conv_general_dilated x10, local copies, waits for them, and re-layouts, local_conv(): lax.conv_general_dilated(volume, kernel, (2, 2, 2), ((0, 0), (pad_rows, p...  17 us
    ppermute x2, waiting for transfers between devices, shifted(): return lax.ppermute(block, axis, route)  16.1 us
    conv_general_dilated x2, matrix products, local_conv(): lax.conv_general_dilated(volume, kernel, (2, 2, 2), ((0, 0), (pad_rows, p...  12.7 us
    select_n x2, other arithmetic, turn_the_things(): g_now = jnp.where(far_arr & local_next == 0, last, high)  11.4 us
    ppermute x2, starting transfers between devices, shifted(): return lax.ppermute(block, axis, route)  9.28 us
  transfers between devices with their start and end apart: 5, of which 5 were waited for; matrix products, arithmetic and copies ran while one was open for 3% of the time, Pallas kernels for 0%

profile of v1, /device:TPU:0, one launch (start us, length us, event | category | flops | bytes accessed | tf_op | source)
XLA Modules:
  0.0 277.3 jit_solution(8228020014091951424)
XLA Ops:
  6.5 0.0 copy-start
  6.5 0.0 all-gather.2.cloned.1.call-start
  6.5 0.0 copy-start.1
  6.5 3.0 %slice.12 = bf16[32,1,8192]{2,1,0:T(2,128)(2,1)S(1)} slice(bf16[32,4,8192]{2,1,0:T(4,128)(2,1)} %param.5), slice={[0:32], [3:4], [0:8192]} | slice | bytes 1048576 | tf_op jit(solution)/shard_map/slice | solution.py:39
  9.6 0.6 copy.67
  10.1 4.9 %collective-permute-start = (bf16[32,1,8192]{2,0,1:T(8,128)(2,1)S(1)}, bf16[32,1,8192]{2,0,1:T(8,128)(2,1)S(1)}, u32[]{:S(2)}, u32[]{:S(2)}) collective-permute-start(bf16[32,1,8192]{2,0,1:T(8,128)(2,1)S(1)} %copy.67), channel_id=1, source_target_pairs={{0,4},{4,8},{8,12},{12,16},{16,20},{20,24},{24,28},{1,5},{5,9},{9,... | collective-permute-start | bytes 1572872 | tf_op jit(solution)/shard_map/ppermute | solution.py:13
  15.0 11.1 %collective-permute-done = bf16[32,1,8192]{2,0,1:T(8,128)(2,1)S(1)} collective-permute-done((bf16[32,1,8192]{2,0,1:T(8,128)(2,1)S(1)}, bf16[32,1,8192]{2,0,1:T(8,128)(2,1)S(1)}, u32[]{:S(2)}, u32[]{:S(2)}) %collective-permute-start) | collective-permute-done | bytes 524320 | tf_op jit(solution)/shard_map/ppermute | solution.py:13
  26.2 0.0 copy-done.1
  26.2 1.2 constant_dynamic-update-slice_fusion
  27.4 0.1 collective-permute-start.1
  27.5 0.0 copy-start.3
  27.5 5.0 %collective-permute-done.1 = bf16[32,5,8192]{2,0,1:T(8,128)(2,1)} collective-permute-done((bf16[32,5,8192]{2,0,1:T(8,128)(2,1)S(1)}, bf16[32,5,8192]{2,0,1:T(8,128)(2,1)}, u32[]{:S(2)}, u32[]{:S(2)}) %collective-permute-start.1) | collective-permute-done | bytes 2621472 | tf_op jit(solution)/shard_map/ppermute | solution.py:53
  32.5 6.4 %maximum_select_fusion.2 = bf16[64,5,8192]{2,0,1:T(8,128)(2,1)} fusion(bf16[32,5,8192]{2,0,1:T(8,128)(2,1)} %collective-permute-done.1, bf16[32,5,8192]{2,0,1:T(8,128)(2,1)S(1)} %constant_dynamic-update-slice_fusion, pred[]{:T(512)S(6)} %eq.7), kind=kLoop, calls=%fused_computation.12 | loop fusion | flops 23592960 | bytes 10485761 | tf_op jit(solution)/shard_map/jit(_where)/select_n | solution.py:56
  38.9 1.5 collective-permute-start.2
  40.4 0.0 copy-done.3
  40.4 0.7 copy.63
  41.2 2.5 copy.64
  43.6 4.9 %fusion.8 = bf16[1,64,5,64,128]{4,3,1,2,0:T(8,128)(2,1)S(1)} fusion(bf16[32,5,64,128]{3,2,0,1:T(8,128)(2,1)S(1)} %bitcast.57, bf16[32,5,64,128]{3,2,0,1:T(8,128)(2,1)S(1)} %bitcast.56, pred[]{:T(512)S(6)} %eq.7), kind=kLoop, calls=%fused_computation.11 | loop fusion | flops 7864320 | bytes 10485761 | tf_op jit(solution)/shard_map/concatenate | solution.py:54
  48.5 105.8 %collective-permute-done.2 = bf16[64,5,8192]{2,0,1:T(8,128)(2,1)} collective-permute-done((bf16[64,5,8192]{2,0,1:T(8,128)(2,1)}, bf16[64,5,8192]{2,0,1:T(8,128)(2,1)}, u32[]{:S(2)}, u32[]{:S(2)}) %collective-permute-start.2) | collective-permute-done | bytes 5242912 | tf_op jit(solution)/shard_map/ppermute | solution.py:53
  154.3 4.0 %copy.65 = bf16[40,8,64,128]{3,2,1,0:T(8,128)(2,1)S(1)} copy(bf16[40,8,64,128]{3,1,2,0:T(8,128)(2,1)} %bitcast.28) | data formatting | bytes 10485760
  158.3 5.0 %fusion.5 = bf16[128,5,64,1,128]{4,2,0,1,3:T(8,128)(2,1)} fusion(bf16[1,64,5,64,128]{4,3,1,2,0:T(8,128)(2,1)S(1)} %bitcast.52, bf16[1,64,5,64,128]{4,3,1,2,0:T(8,128)(2,1)S(1)} %fusion.8, pred[]{:T(512)S(6)} %eq.6), kind=kLoop, calls=%fused_computation.6 | loop fusion | flops 15728640 | bytes 20971520 | tf_op jit(solution)/shard_map/jit(_where)/select_n | solution.py:56
  163.3 16.8 %copy.61 = bf16[128,5,64,1,128]{0,2,4,1,3:T(8,128)(2,1)} copy(bf16[128,5,64,1,128]{4,2,0,1,3:T(8,128)(2,1)} %fusion.5) | data formatting | bytes 20971520
  180.1 6.4 %pad.clone = bf16[128,5,64,1,144]{0,2,4,1,3:T(8,128)(2,1)S(1)} pad(bf16[128,5,64,1,128]{0,2,4,1,3:T(8,128)(2,1)} %copy.61, bf16[]{:T(256)} %constant.5), padding=0_0x0_0x0_0x0_0x1_15 | pad | bytes 22282242 | tf_op jit(solution)/shard_map/jit(_where)/select_n | solution.py:56
  186.5 0.0 copy-start.2
  186.5 0.0 copy-start.5
  186.5 8.6 %copy.51 = bf16[128,5,64,1,8,18]{0,4,5,2,1,3:T(8,128)(2,1)S(1)} copy(bf16[128,5,64,1,8,18]{0,2,5,4,1,3:T(8,128)(2,1)S(1)} %bitcast.51) | data formatting | bytes 23592960 | tf_op jit(solution)/shard_map/conv_general_dilated | solution.py:21
  195.2 0.3 slice.13
  195.5 0.0 copy-done.2
  195.5 0.0 copy-done.5
  195.5 10.2 %fusion.14 = f32[2,32,8,9,64]{4,2,3,1,0:T(8,128)} fusion(bf16[3,3,3,64,128]{4,3,2,1,0:T(8,128)(2,1)S(1)} %bitcast.61, bf16[128,5,64,1,7,2]{0,4,5,2,1,3:T(8,128)(2,1)S(1)} %slice.13, bf16[128,5,64,1,8,18]{0,4,5,2,1,3:T(8,128)(2,1)S(1)} %copy.51, pred[8,9]{0,1:T(8,128)(4,1)S(1)} %copy-done.5), kind=kOutput, calls=%fused_computation.19 | convolution fusion | flops 2056814592 | bytes 14565448 | tf_op jit(solution)/shard_map/conv_general_dilated | solution.py:21
  205.8 2.1 copy.52
  207.9 0.2 slice_bitcast_fusion
  208.1 0.0 copy-start.4
  208.1 3.1 %copy.53 = f32[1,64,2,32,64]{4,3,1,2,0:T(8,128)} copy(f32[1,64,2,32,64]{1,3,4,2,0:T(8,128)S(1)} %slice_bitcast_fusion) | data formatting | bytes 2097152 | tf_op jit(solution)/shard_map/conv_general_dilated | solution.py:21
  211.1 2.1 squeeze.6
  213.2 0.2 fusion.20
  213.5 4.4 %collective-permute-start.3 = (bf16[64,1,2048]{2,0,1:T(8,128)(2,1)S(1)}, bf16[64,1,2048]{2,0,1:T(8,128)(2,1)S(1)}, u32[]{:S(2)}, u32[]{:S(2)}) collective-permute-start(bf16[64,1,2048]{2,0,1:T(8,128)(2,1)S(1)} %slice.15), channel_id=1, source_target_pairs={{0,4},{4,8},{8,12},{12,16},{16,20},{20,24},{24,28},{1,5},{5,9},{9,... | collective-permute-start | bytes 786440 | tf_op jit(solution)/shard_map/ppermute | solution.py:13
  217.9 5.0 %collective-permute-done.3 = bf16[64,1,2048]{2,0,1:T(8,128)(2,1)S(1)} collective-permute-done((bf16[64,1,2048]{2,0,1:T(8,128)(2,1)S(1)}, bf16[64,1,2048]{2,0,1:T(8,128)(2,1)S(1)}, u32[]{:S(2)}, u32[]{:S(2)}) %collective-permute-start.3) | collective-permute-done | bytes 262176 | tf_op jit(solution)/shard_map/ppermute | solution.py:13
  222.9 1.0 pad_maximum_fusion
  223.9 0.0 all-gather.2.cloned.1.call-update
  223.9 0.0 copy-done.4
  223.9 31.8 %all-gather.2.cloned.1.call-done = bf16[256,3,2048]{2,0,1:T(8,128)(2,1)} async-done(((bf16[64,3,2048]{2,0,1:T(8,128)(2,1)}), bf16[256,3,2048]{2,0,1:T(8,128)(2,1)}) %all-gather.2.cloned.1.call-update) | async-done | bytes 3145744 | tf_op jit(solution)/shard_map/all_gather | solution.py:69
  255.7 4.6 %copy.54 = bf16[256,3,2048]{0,2,1:T(8,128)(2,1)} copy(bf16[256,3,2048]{2,0,1:T(8,128)(2,1)} %all-gather.2.cloned.1.call-done) | data formatting | bytes 6291456 | tf_op jit(solution)/shard_map/all_gather | solution.py:69
  260.3 3.7 %copy.62 = bf16[256,3,32,1,64]{0,2,4,1,3:T(8,128)(2,1)S(1)} copy(bf16[256,3,32,1,64]{0,4,2,1,3:T(8,128)(2,1)} %bitcast.55) | data formatting | bytes 6291456
  264.0 0.4 pad.2.clone
  264.4 0.0 copy-start.6
  264.5 2.3 copy.57
  266.7 0.2 slice.16
  266.9 0.0 copy-done
  266.9 0.0 copy-done.6
  267.0 2.5 fusion.17
  269.4 0.1 copy.58
  269.5 0.1 copy.59
  269.6 0.1 copy.60
  269.7 0.7 fusion.21
  (5 shorter events, 0.1 us)
Async XLA Ops:
  6.5 260.4 %copy-start = (bf16[27,64,256]{2,1,0:T(8,128)(2,1)S(1)}, bf16[27,64,256]{2,1,0:T(8,128)(2,1)}, u32[]{:S(2)}) copy-start(bf16[27,64,256]{2,1,0:T(8,128)(2,1)} %param.8) | copy-start | bytes 2654212
  6.5 249.2 %all-gather.2.cloned.1.call-start = ((), (), s32[]{:S(2)}) async-start(), calls=%async_computation | async-start | bytes 3932160 | tf_op jit(solution)/shard_map/all_gather | solution.py:69
  6.5 19.7 %copy-start.1 = (bf16[32,4,8192]{2,1,0:T(4,128)(2,1)S(1)}, bf16[32,4,8192]{2,1,0:T(4,128)(2,1)}, u32[]{:S(2)}) copy-start(bf16[32,4,8192]{2,1,0:T(4,128)(2,1)} %param.5) | copy-start | bytes 6291460
  10.1 16.0 %collective-permute-start = (bf16[32,1,8192]{2,0,1:T(8,128)(2,1)S(1)}, bf16[32,1,8192]{2,0,1:T(8,128)(2,1)S(1)}, u32[]{:S(2)}, u32[]{:S(2)}) collective-permute-start(bf16[32,1,8192]{2,0,1:T(8,128)(2,1)S(1)} %copy.67), channel_id=1, source_target_pairs={{0,4},{4,8},{8,12},{12,16},{16,20},{20,24},{24,28},{1,5},{5,9},{9,... | collective-permute-start | bytes 1572872 | tf_op jit(solution)/shard_map/ppermute | solution.py:13
  27.4 5.1 %collective-permute-start.1 = (bf16[32,5,8192]{2,0,1:T(8,128)(2,1)S(1)}, bf16[32,5,8192]{2,0,1:T(8,128)(2,1)}, u32[]{:S(2)}, u32[]{:S(2)}) collective-permute-start(bf16[32,5,8192]{2,0,1:T(8,128)(2,1)S(1)} %constant_dynamic-update-slice_fusion), channel_id=1, source_target_pairs={{0,1},{1,0},{2,3},{3,2},{4,5},{5,4},{6,7},{7,6},{8,9},{9,8},{10,11... | collective-permute-start | bytes 7864328 | tf_op jit(solution)/shard_map/ppermute | solution.py:53
  27.5 13.0 %copy-start.3 = (bf16[64]{0:T(256)(128)(2,1)S(1)}, bf16[64]{0:T(256)(128)(2,1)}, u32[]{:S(2)}) copy-start(bf16[64]{0:T(256)(128)(2,1)} %param.7) | copy-start | bytes 388
  38.9 115.4 %collective-permute-start.2 = (bf16[64,5,8192]{2,0,1:T(8,128)(2,1)}, bf16[64,5,8192]{2,0,1:T(8,128)(2,1)}, u32[]{:S(2)}, u32[]{:S(2)}) collective-permute-start(bf16[64,5,8192]{2,0,1:T(8,128)(2,1)} %maximum_select_fusion.2), channel_id=1, source_target_pairs={{0,2},{1,3},{2,0},{3,1},{4,6},{5,7},{6,4},{7,5},{8,10},{9,11},{10,... | collective-permute-start | bytes 15728648 | tf_op jit(solution)/shard_map/ppermute | solution.py:53
  186.5 9.0 %copy-start.2 = (bf16[27,64,128]{2,1,0:T(8,128)(2,1)S(1)}, bf16[27,64,128]{2,1,0:T(8,128)(2,1)}, u32[]{:S(2)}) copy-start(bf16[27,64,128]{2,1,0:T(8,128)(2,1)} %param.6) | copy-start | bytes 1327108
  186.5 9.0 %copy-start.5 = (pred[8,9]{0,1:T(8,128)(4,1)S(1)}, pred[8,9]{0,1:T(8,128)(4,1)}, u32[]{:S(2)}) copy-start(pred[8,9]{0,1:T(8,128)(4,1)} %constant.26) | copy-start | bytes 220
  208.1 15.8 %copy-start.4 = (bf16[64]{0:T(256)(128)(2,1)S(1)}, bf16[64]{0:T(256)(128)(2,1)}, u32[]{:S(2)}) copy-start(bf16[64]{0:T(256)(128)(2,1)} %param.9) | copy-start | bytes 388
  213.5 9.4 %collective-permute-start.3 = (bf16[64,1,2048]{2,0,1:T(8,128)(2,1)S(1)}, bf16[64,1,2048]{2,0,1:T(8,128)(2,1)S(1)}, u32[]{:S(2)}, u32[]{:S(2)}) collective-permute-start(bf16[64,1,2048]{2,0,1:T(8,128)(2,1)S(1)} %slice.15), channel_id=1, source_target_pairs={{0,4},{4,8},{8,12},{12,16},{16,20},{20,24},{24,28},{1,5},{5,9},{9,... | collective-permute-start | bytes 786440 | tf_op jit(solution)/shard_map/ppermute | solution.py:13
  264.4 2.5 copy-start.6
Sparse Core Ops, SparseCore 0:
  224.0 31.6 all-gather.1
